TPU v7x, 32 devices: a whole 2x2x4 slice. The times are simulated.
32 devices in a mesh: dp: 8 (over z, y), space: 4 (over x, core).
Axes of the slice: x: 2, y: 2, z: 4, core: 2. Of those that a mesh axis runs over, the one named last changes fastest.
Arguments:
- volume: bfloat16 [8, 4, 32, 32, 32], P('dp', None, 'space'), may hold values from -6 to 6
- cotangent: bfloat16 [8, 64, 512], P('dp', None, 'space'), may hold values from -6 to 6
- conv_one: bfloat16 [32, 4, 3, 3, 3], replicated, may hold values from -0.625 to 0.625
- conv_two: bfloat16 [64, 32, 3, 3, 3], replicated, may hold values from -0.21875 to 0.21875
Outputs:
- out_two: bfloat16 [8, 64, 512], P('dp', None, 'space')
- grad_pre: bfloat16 [8, 32, 4096], P('dp', None, 'space')
- update_one: float32 [3456], replicated
- update_two: float32 [55296], replicated
All inputs are finite; a program needn't handle non-finite values.
Results may differ from a plain program's by a relative error of at most 0.0057.
Values may be sent and summed in bfloat16 or wider, within the bound.
A program may use at most 64 MiB of HBM per device.

v0:
```python
import jax
import jax.numpy as jnp
from jax import lax
from jax.sharding import PartitionSpec as P

damp_input = 0.1
damp_grad = 0.03


def passed_along(value, axis, steps):
    count = lax.axis_size(axis)
    leading, last = (max(0, -steps), min(count, count - steps))
    return lax.ppermute(value, axis, [(source, source + steps) for source in range(leading, last)])


def tap_stack(padded, out_depth, out_rows, out_cols):
    pieces = []
    for depth_tap in range(3):
        for row_tap in range(3):
            for col_tap in range(3):
                pieces.append(
                    padded[
                        :,
                        depth_tap : depth_tap + 2 * out_depth : 2,
                        row_tap : row_tap + 2 * out_rows : 2,
                        col_tap : col_tap + 2 * out_cols : 2,
                    ]
                )
    stacked = jnp.stack(pieces, axis=1)
    return stacked.reshape(stacked.shape[0] * 27, -1)


def spread_taps(columns, channels, out_depth, out_rows, out_cols):
    pieces = columns.reshape(channels, 27, out_depth, out_rows, out_cols)
    canvas = jnp.zeros(
        (channels, 2 * out_depth + 1, 2 * out_rows + 1, 2 * out_cols + 1), jnp.float32
    )
    for depth_tap in range(3):
        for row_tap in range(3):
            for col_tap in range(3):
                tap_number = depth_tap * 9 + row_tap * 3 + col_tap
                canvas = canvas.at[
                    :,
                    depth_tap : depth_tap + 2 * out_depth : 2,
                    row_tap : row_tap + 2 * out_rows : 2,
                    col_tap : col_tap + 2 * out_cols : 2,
                ].add(pieces[:, tap_number])
    return canvas


def silu_slope(pre_act):
    sigmoid_val = jax.nn.sigmoid(pre_act)
    return sigmoid_val * (1.0 + pre_act * (1.0 - sigmoid_val))


def damped_solve(matrix, rhs_terms):
    lower_factor = jnp.linalg.cholesky(matrix)
    return jax.scipy.linalg.cho_solve((lower_factor, True), rhs_terms)


def precondition(gram_in, gram_out, grad_sum, total_rows):
    in_mat = gram_in / total_rows + damp_input * jnp.eye(gram_in.shape[0], dtype=jnp.float32)
    out_mat = gram_out / total_rows + damp_grad * jnp.eye(gram_out.shape[0], dtype=jnp.float32)
    mean_grad = grad_sum / total_rows
    half_solved = damped_solve(in_mat, mean_grad.T).T
    return (damped_solve(out_mat, half_solved), mean_grad)


def on_device(volume, cotangent, conv_one, conv_two):
    local_volume = volume[0]
    cot_flat = cotangent[0]
    depth_len, row_count, col_count = (
        local_volume.shape[1],
        local_volume.shape[2],
        local_volume.shape[3],
    )
    width_one = conv_one.shape[0]
    width_two = conv_two.shape[0]
    weight_one = conv_one.reshape(width_one, -1)
    weight_two = conv_two.reshape(width_two, -1)
    lower_plane = passed_along(local_volume[:, depth_len - 1], "space", 1)
    extended = jnp.concatenate([lower_plane[:, None], local_volume], axis=1)
    padded = jnp.pad(extended, ((0, 0), (0, 0), (1, 0), (1, 0)))
    first_cols = tap_stack(padded, depth_len // 2, row_count // 2, col_count // 2)
    pre_one = jnp.dot(weight_one, first_cols, preferred_element_type=jnp.float32)
    act_one = (
        jax.nn.silu(pre_one)
        .astype(jnp.bfloat16)
        .reshape(width_one, depth_len // 2, row_count // 2, col_count // 2)
    )
    lower_act = passed_along(act_one[:, depth_len // 2 - 1], "space", 1)
    extended_two = jnp.concatenate([lower_act[:, None], act_one], axis=1)
    padded_two = jnp.pad(extended_two, ((0, 0), (0, 0), (1, 0), (1, 0)))
    second_cols = tap_stack(padded_two, depth_len // 4, row_count // 4, col_count // 4)
    out_two = jnp.dot(weight_two, second_cols, preferred_element_type=jnp.float32).astype(
        jnp.bfloat16
    )
    back_cols = jnp.dot(weight_two.T, cot_flat, preferred_element_type=jnp.float32)
    canvas = spread_taps(back_cols, width_one, depth_len // 4, row_count // 4, col_count // 4)
    grad_act = canvas[:, 1:, 1:, 1:]
    upper_part = passed_along(canvas[:, 0, 1:, 1:].astype(jnp.bfloat16), "space", -1).astype(
        jnp.float32
    )
    grad_act = grad_act.at[:, -1].add(upper_part)
    grad_pre = (grad_act.reshape(width_one, -1) * silu_slope(pre_one)).astype(jnp.bfloat16)
    in_one = jnp.dot(first_cols, first_cols.T, preferred_element_type=jnp.float32)
    gram_one = jnp.dot(grad_pre, grad_pre.T, preferred_element_type=jnp.float32)
    grad_one = jnp.dot(grad_pre, first_cols.T, preferred_element_type=jnp.float32)
    in_two = jnp.dot(second_cols, second_cols.T, preferred_element_type=jnp.float32)
    gram_two = jnp.dot(cot_flat, cot_flat.T, preferred_element_type=jnp.float32)
    grad_two = jnp.dot(cot_flat, second_cols.T, preferred_element_type=jnp.float32)
    summed = lax.psum((in_two, in_one, gram_one, grad_one, gram_two, grad_two), ("dp", "space"))
    total_in_two, total_in_one, total_gram_one, total_grad_one, total_gram_two, total_grad_two = (
        summed
    )
    device_count = lax.axis_size("dp") * lax.axis_size("space")
    rows_one = first_cols.shape[1] * device_count
    rows_two = cot_flat.shape[1] * device_count
    step_one, mean_one = precondition(total_in_one, total_gram_one, total_grad_one, rows_one)
    step_two, mean_two = precondition(total_in_two, total_gram_two, total_grad_two, rows_two)
    quad_form = jnp.sum(step_one * mean_one) + jnp.sum(step_two * mean_two)
    factor = jnp.sqrt((step_one.size + step_two.size) / quad_form)
    update_one = (factor * step_one).reshape(-1)
    update_two = (factor * step_two).reshape(-1)
    return (out_two[None], grad_pre[None], update_one, update_two)


def solution(mesh):
    in_specs = (P("dp", None, "space", None, None), P("dp", None, "space"), P(), P())
    out_specs = (P("dp", None, "space"), P("dp", None, "space"), P(), P())
    return jax.shard_map(
        on_device, mesh=mesh, in_specs=in_specs, out_specs=out_specs, check_vma=False
    )
```

profile of v0, /device:TPU:0, one launch (start us, length us, event | category | flops | bytes accessed | tf_op | source)
XLA Modules:
  0.0 933.9 jit_solution(1185647925688393770)
XLA Ops:
  21.5 8.7 scatter_fusion.1
  38.9 8.7 scatter_fusion.3
  73.7 8.7 scatter_fusion.7
  91.1 8.7 scatter_fusion.9
  117.1 8.9 scatter_fusion.12
  221.7 9.1 scatter_fusion.24
  390.8 104.5 %all-reduce.10.cloned.1.call-done = (f32[108,108]{1,0:T(8,128)}, f32[32,108]{1,0:T(8,128)}, f32[32,32]{1,0:T(8,128)}, f32[64,64]{1,0:T(8,128)}) async-done(((f32[108,108]{1,0:T(8,128)}, f32[32,108]{1,0:T(8,128)}, f32[32,32]{1,0:T(8,128)}, f32[64,64]{1,0:T(8,128)}), (f32[108,108]{1,0:T(8,128)}, f32[32,108]{1,0:T(8,128)}, f32[32,32]{1,0:T(8,128)}, f32[64,64]{1,0:T(8,128)})) %all-reduce.10.cloned.1.call-update) | async-done | bytes 80976 | tf_op jit(solution)/shard_map/psum | solution.py:112
  497.0 9.9 %cholesky.246 = f32[108,108]{1,0:T(8,128)S(1)} custom-call(f32[108,108]{1,0:T(8,128)S(1)} %fusion.98), custom_call_target="Cholesky" | custom-call | tf_op jit(solution)/shard_map/jit(cholesky)/cholesky | solution.py:57
  542.7 97.4 %all-reduce.12.cloned.1.call-done = (f32[864,864]{1,0:T(8,128)}, f32[64,864]{1,0:T(8,128)}) async-done(((f32[864,864]{1,0:T(8,128)}, f32[64,864]{1,0:T(8,128)}), (f32[864,864]{1,0:T(8,128)}, f32[64,864]{1,0:T(8,128)})) %all-reduce.12.cloned.1.call-update) | async-done | bytes 3207184 | tf_op jit(solution)/shard_map/psum | solution.py:112
  652.4 11.7 %cholesky.269 = f32[128,128]{1,0:T(8,128)S(1)} custom-call(f32[128,128]{1,0:T(8,128)S(1)} %cholesky.607), custom_call_target="Cholesky" | custom-call | tf_op jit(solution)/shard_map/jit(cholesky)/cholesky | solution.py:57
  665.1 9.8 %custom-call.91 = f32[1,128,128]{1,2,0:T(8,128)S(1)} custom-call(f32[1,128,128]{2,1,0:T(8,128)S(1)} %get-tuple-element.85), custom_call_target="InvertDiagBlocksLowerTriangular" | custom-call | tf_op jit(solution)/shard_map/jit(cholesky)/cholesky | solution.py:57
  678.4 12.5 %cholesky.492 = f32[128,128]{1,0:T(8,128)S(1)} custom-call(f32[128,128]{1,0:T(8,128)} %cholesky.611), custom_call_target="Cholesky" | custom-call | tf_op jit(solution)/shard_map/jit(cholesky)/cholesky | solution.py:57
  691.6 11.0 %custom-call.92 = f32[1,128,128]{1,2,0:T(8,128)S(1)} custom-call(f32[1,128,128]{2,1,0:T(8,128)} %get-tuple-element.82), custom_call_target="InvertDiagBlocksLowerTriangular" | custom-call | tf_op jit(solution)/shard_map/jit(cholesky)/cholesky | solution.py:57
  704.7 11.7 %cholesky.513 = f32[128,128]{1,0:T(8,128)S(1)} custom-call(f32[128,128]{1,0:T(8,128)S(1)} %cholesky.616), custom_call_target="Cholesky" | custom-call | tf_op jit(solution)/shard_map/jit(cholesky)/cholesky | solution.py:57
  716.5 9.8 %custom-call.93 = f32[1,128,128]{1,2,0:T(8,128)S(1)} custom-call(f32[1,128,128]{2,1,0:T(8,128)S(1)} %get-tuple-element.79), custom_call_target="InvertDiagBlocksLowerTriangular" | custom-call | tf_op jit(solution)/shard_map/jit(cholesky)/cholesky | solution.py:57
  728.3 11.9 %cholesky.532 = f32[128,128]{1,0:T(8,128)S(1)} custom-call(f32[128,128]{1,0:T(8,128)S(1)} %cholesky.621), custom_call_target="Cholesky" | custom-call | tf_op jit(solution)/shard_map/jit(cholesky)/cholesky | solution.py:57
  740.2 9.8 %custom-call.94 = f32[1,128,128]{1,2,0:T(8,128)S(1)} custom-call(f32[1,128,128]{2,1,0:T(8,128)S(1)} %get-tuple-element.76), custom_call_target="InvertDiagBlocksLowerTriangular" | custom-call | tf_op jit(solution)/shard_map/jit(cholesky)/cholesky | solution.py:57
  752.0 11.7 %cholesky.551 = f32[128,128]{1,0:T(8,128)S(1)} custom-call(f32[128,128]{1,0:T(8,128)S(1)} %cholesky.626), custom_call_target="Cholesky" | custom-call | tf_op jit(solution)/shard_map/jit(cholesky)/cholesky | solution.py:57
  763.8 9.8 %custom-call.95 = f32[1,128,128]{1,2,0:T(8,128)S(1)} custom-call(f32[1,128,128]{2,1,0:T(8,128)S(1)} %get-tuple-element.73), custom_call_target="InvertDiagBlocksLowerTriangular" | custom-call | tf_op jit(solution)/shard_map/jit(cholesky)/cholesky | solution.py:57
  775.4 11.9 %cholesky.571 = f32[128,128]{1,0:T(8,128)S(1)} custom-call(f32[128,128]{1,0:T(8,128)S(1)} %cholesky.631), custom_call_target="Cholesky" | custom-call | tf_op jit(solution)/shard_map/jit(cholesky)/cholesky | solution.py:57
  787.4 9.8 %custom-call.96 = f32[1,128,128]{1,2,0:T(8,128)S(1)} custom-call(f32[1,128,128]{2,1,0:T(8,128)S(1)} %get-tuple-element.70), custom_call_target="InvertDiagBlocksLowerTriangular" | custom-call | tf_op jit(solution)/shard_map/jit(cholesky)/cholesky | solution.py:57
  798.6 8.8 cholesky.592
  818.4 18.1 %while.2 = (s32[]{:T(128)}, f32[864,864]{1,0:T(8,128)}, s32[6,2]{0,1:T(2,128)S(1)}, f32[6,128,128]{2,1,0:T(8,128)S(1)}, s32[]{:T(128)}) while((s32[]{:T(128)}, f32[864,864]{1,0:T(8,128)}, s32[6,2]{0,1:T(2,128)S(1)}, f32[6,128,128]{2,1,0:T(8,128)S(1)}, s32[]{:T(128)}) %tuple.123), condition=%wide.while_cond.1, body=%wide.while_body.1.sunk | while | flops 2 | bytes 131189 | solution.py:58
  838.4 69.8 %custom-call.97 = f32[7,128,128]{1,2,0:T(8,128)S(1)} custom-call(f32[7,128,128]{2,1,0:T(8,128)} %pad_maximum_fusion), custom_call_target="InvertDiagBlocksLowerTriangular" | custom-call | tf_op jit(solution)/shard_map/jit(_cho_solve)/triangular_solve | solution.py:58
  (374 shorter events, 437.0 us)
Async XLA Ops:
  7.2 488.1 %all-reduce.10.cloned.1.call-start = ((), (), s32[]{:S(2)}) async-start(), calls=%async_computation | async-start | bytes 245760 | tf_op jit(solution)/shard_map/psum | solution.py:112
  239.5 10.6 %copy-start.8 = (bf16[1,4,8,32,32]{4,3,2,1,0:T(8,128)(2,1)S(1)}, bf16[1,4,8,32,32]{4,3,2,1,0:T(8,128)(2,1)}, u32[]{:S(2)}) copy-start(bf16[1,4,8,32,32]{4,3,2,1,0:T(8,128)(2,1)} %param.6) | copy-start | bytes 196612
  239.5 13.7 %copy-start.10 = (bf16[1,64,128]{2,1,0:T(8,128)(2,1)S(1)}, bf16[1,64,128]{2,1,0:T(8,128)(2,1)}, u32[]{:S(2)}) copy-start(bf16[1,64,128]{2,1,0:T(8,128)(2,1)} %param.7) | copy-start | bytes 49156
  239.5 15.7 %copy-start.12 = (bf16[32,4,3,3,3]{0,1,4,3,2:T(4,128)(2,1)S(1)}, bf16[32,4,3,3,3]{0,1,4,3,2:T(4,128)(2,1)}, u32[]{:S(2)}) copy-start(bf16[32,4,3,3,3]{0,1,4,3,2:T(4,128)(2,1)} %param.8) | copy-start | bytes 20740
  248.8 112.8 %collective-permute-start.2 = (bf16[32,16,16]{0,2,1:T(8,128)(2,1)}, bf16[32,16,16]{0,2,1:T(8,128)(2,1)}, u32[]{:S(2)}, u32[]{:S(2)}) collective-permute-start(bf16[32,16,16]{0,2,1:T(8,128)(2,1)} %fusion.66), channel_id=1, source_target_pairs={{1,0},{2,1},{3,2},{5,4},{6,5},{7,6},{9,8},{10,9},{11,10},{13,12},{... | collective-permute-start | bytes 49160 | tf_op jit(solution)/shard_map/ppermute | solution.py:13
  250.2 5.1 collective-permute-start
  362.8 20.5 %copy-start.4 = (bf16[32,1024]{1,0:T(8,128)(2,1)}, bf16[32,1024]{1,0:T(8,128)(2,1)S(1)}, u32[]{:S(2)}) copy-start(bf16[32,1024]{1,0:T(8,128)(2,1)S(1)} %get-tuple-element.67) | copy-start | bytes 196612
  363.0 6.1 collective-permute-start.1
  369.0 271.0 %all-reduce.12.cloned.1.call-start = ((), (), s32[]{:S(2)}) async-start(), calls=%async_computation.1 | async-start | bytes 6651904 | tf_op jit(solution)/shard_map/psum | solution.py:112
  643.9 4.6 copy-start
  650.8 1.6 copy-start.3
  652.4 12.0 %copy-start.5 = (f32[64,864]{1,0:T(8,128)S(1)}, f32[64,864]{1,0:T(8,128)}, u32[]{:S(2)}) copy-start(f32[64,864]{1,0:T(8,128)} %get-tuple-element.37) | copy-start | bytes 663556
  816.4 0.9 copy-start.13
  816.4 1.9 copy-start.7
  816.5 20.1 %copy-start.9 = (f32[128,32]{1,0:T(8,128)S(1)}, f32[128,32]{1,0:T(8,128)}, u32[]{:S(2)}) copy-start(f32[128,32]{1,0:T(8,128)} %pad_convert_fusion) | copy-start | bytes 49156
  816.7 1.7 copy-start.1
  836.5 78.4 %copy-start.2 = (f32[864,864]{1,0:T(8,128)S(1)}, f32[864,864]{1,0:T(8,128)}, u32[]{:S(2)}) copy-start(f32[864,864]{1,0:T(8,128)} %get-tuple-element.214) | copy-start | bytes 8957956
  913.3 8.2 copy-start.11
  914.9 7.1 copy-start.6
Sparse Core Ops, SparseCore 0:
  369.2 126.0 all-reduce.9
  500.9 139.1 all-reduce.11
where the time goes:
time: 946 us; the launch traced here: 934 us
  other arithmetic  507 us (54%)
  waiting for transfers between devices  202 us (21%)
  local copies, waits for them, and re-layouts  157 us (17%)
  matrix products  37.8 us (4%)
  between operations  22.1 us (2%)
    scatter-add x27, other arithmetic, spread_taps(): canvas = canvas.at[:, depth_tap:depth_tap + 2 * out_depth:2, row_tap:row_...  235 us
    psum x2, waiting for transfers between devices, on_device(): lax.psum((in_two, in_one, gram_one, grad_one, gram_two, grad_two), ('dp',...  202 us
    another operation x36, other arithmetic, damped_solve(): lower_factor = jnp.linalg.cholesky(matrix)  166 us
    another operation x13, other arithmetic, damped_solve(): return jax.scipy.linalg.cho_solve((lower_factor, True), rhs_terms)  91.3 us
    slice x54, local copies, waits for them, and re-layouts, tap_stack(): padded[:, depth_tap:depth_tap + 2 * out_depth:2, row_tap:row_tap + 2 * ou...  90.9 us
    unnamed x95, local copies, waits for them, and re-layouts  27 us
  transfers between devices with their start and end apart: 5, of which 2 were waited for; matrix products, arithmetic and copies ran while one was open for 19% of the time, Pallas kernels for 0%

commit v1 on v0

v1 whole, which is shorter than its diff:
```python
import jax
import jax.numpy as jnp
import numpy as np
from jax import lax
from jax.experimental import pallas as pl
from jax.experimental.pallas import tpu as pltpu
from jax.sharding import PartitionSpec as P

damp_input = 0.1
damp_grad = 0.03
TOLERANCE = 1e-6
MAX_STEPS = 5000
CELLS = 128
PLANE = 64
BLOCKS_ONE = [(sd, sh, sw) for sd in (0, 1) for sh in (0, 1) for sw in (0, 1)]
TAPS = [(a, b, e) for a in range(3) for b in range(3) for e in range(3)]
PHASES = [(d, h, w) for d in (0, 1) for h in (0, 1) for w in (0, 1)]
SUBROWS = 896


def block_rows():
    table, row = {}, 0
    for sd, sh, sw in BLOCKS_ONE:
        for md in (3,) if sd else range(4):
            for mh in (3,) if sh else range(4):
                for mw in range(4):
                    for c in range(4):
                        table[(sd, sh, sw, md, mh, mw, c)] = row
                        row += 1
    return table


def selection():
    table = block_rows()
    sel = np.zeros((8 * 128, SUBROWS), np.float32)
    for ph, (dp, hp, wp) in enumerate(PHASES):
        for c in range(4):
            for t, (a, b, e) in enumerate(TAPS):
                offs = [2 * dp + a - 1, 2 * hp + b - 1, 2 * wp + e - 1]
                sh = [int(o < 0) for o in offs]
                md = [o % 4 for o in offs]
                sel[ph * 128 + c * 27 + t, table[(*sh, *md, c)]] = 1.0
    return sel


def dot(left, right):
    return jnp.dot(left, right, preferred_element_type=jnp.float32)


def dot_t(left, right):
    return lax.dot_general(left, right, (((1,), (1,)), ((), ())), preferred_element_type=jnp.float32)


def patches_two(act, p_idx, q_idx, tap):
    a, b, e = tap
    ph = 4 * (a != 1) + 2 * (b != 1) + (e != 1)
    shift = 64 * (a == 0) + 8 * (b == 0) + (e == 0)
    rows = act[ph * 32 : ph * 32 + 32]
    if shift:
        rows = pltpu.roll(rows, shift, 1)
    rows = rows[:, CELLS:]
    if b == 0:
        rows = jnp.where(p_idx == 0, 0.0, rows)
    if e == 0:
        rows = jnp.where(q_idx == 0, 0.0, rows)
    return rows.astype(jnp.bfloat16)


def local_kernel(
    v_ref, c_ref, sel_ref, w1_ref, w2_ref, w2t_ref,
    out_ref, e1_ref, in_two_ref, grad_two_ref, small_ref,
    x_ref, p1_ref, p2_ref,
):
    lane = lax.broadcasted_iota(jnp.int32, (256, 256), 1)
    p_all = (lane // 8) % 8
    q_all = lane % 8
    vol = v_ref[...].astype(jnp.float32)
    row = 0
    for sd, sh, sw in BLOCKS_ONE:
        base = vol[192:] if sd else vol
        shift = 64 * sd + 8 * sh + sw
        if shift:
            base = pltpu.roll(base, shift, 1)
        if sh:
            base = jnp.where(p_all[: base.shape[0]] == 0, 0.0, base)
        if sw:
            base = jnp.where(q_all[: base.shape[0]] == 0, 0.0, base)
        base = base.astype(jnp.bfloat16)
        if sh:
            for md in range(base.shape[0] // 64):
                x_ref[row : row + 16] = base[md * 64 + 48 : md * 64 + 64]
                row += 16
        else:
            x_ref[row : row + base.shape[0]] = base
            row += base.shape[0]
    x_ref[row:] = jnp.zeros((SUBROWS - row, 256), jnp.bfloat16)
    p1_ref[...] = dot(sel_ref[...], x_ref[...]).astype(jnp.bfloat16)
    pre = [dot(w1_ref[...], p1_ref[ph * 128 : ph * 128 + 128]) for ph in range(8)]
    pre = jnp.concatenate(pre, axis=0)
    sig = 1.0 / (1.0 + jnp.exp(-pre))
    act = (pre * sig).astype(jnp.bfloat16).astype(jnp.float32)

    p_own, q_own = p_all[:32, :CELLS], q_all[:32, :CELLS]
    for t, tap in enumerate(TAPS):
        p2_ref[t * 32 : t * 32 + 32] = patches_two(act, p_own, q_own, tap)
    p2 = p2_ref[...]
    out_ref[...] = dot(w2_ref[...], p2).astype(jnp.bfloat16)

    cot = c_ref[...].astype(jnp.float32)
    moved = {}
    for sd, sh, sw in BLOCKS_ONE:
        shift = 64 * sd + 8 * sh + sw
        part = pltpu.roll(cot, 256 - shift, 1) if shift else cot
        part = part[:, :CELLS]
        if sh:
            part = jnp.where(p_all[:64, :CELLS] == 7, 0.0, part)
        if sw:
            part = jnp.where(q_all[:64, :CELLS] == 7, 0.0, part)
        moved[(sd, sh, sw)] = part.astype(jnp.bfloat16)
    grads = [None] * 8
    for t, (a, b, e) in enumerate(TAPS):
        ph = 4 * (a != 1) + 2 * (b != 1) + (e != 1)
        term = dot(w2t_ref[t * 32 : t * 32 + 32], moved[(int(a == 0), int(b == 0), int(e == 0))])
        grads[ph] = term if grads[ph] is None else grads[ph] + term
    grad_act = jnp.concatenate(grads, axis=0)
    pre_own, sig_own = pre[:, CELLS:], sig[:, CELLS:]
    e1 = (grad_act * (sig_own * (1.0 + pre_own * (1.0 - sig_own)))).astype(jnp.bfloat16)
    e1_ref[...] = e1

    in_one = jnp.zeros((128, 128), jnp.float32)
    grad_one = jnp.zeros((32, 128), jnp.float32)
    gram_one = jnp.zeros((32, 32), jnp.float32)
    for ph in range(8):
        p1 = p1_ref[ph * 128 : ph * 128 + 128, CELLS:]
        piece = e1[ph * 32 : ph * 32 + 32]
        in_one += dot_t(p1, p1)
        grad_one += dot_t(piece, p1)
        gram_one += dot_t(piece, piece)
    own_cot = c_ref[:, :CELLS]
    small_ref[...] = jnp.zeros((256, 128), jnp.float32)
    small_ref[0:128] = in_one
    small_ref[128:160] = grad_one
    small_ref[160:192, 0:32] = gram_one
    small_ref[192:256, 0:64] = dot_t(own_cot, own_cot)
    grad_two_ref[...] = dot_t(own_cot, p2)
    in_two_ref[...] = dot_t(p2, p2)


def halves(value):
    high = value.astype(jnp.bfloat16)
    return high, (value - high.astype(jnp.float32)).astype(jnp.bfloat16)


def times(system, direction):
    high, low = halves(direction)
    if system["left"]:
        return dot(system["high"][...], high) + (
            dot(system["high"][...], low) + dot(system["low"][...], high)
        )
    return dot(high, system["high"][...]) + (
        dot(low, system["high"][...]) + dot(high, system["low"][...])
    )


def conjugate_gradients(systems):
    def total(system, value):
        return jnp.sum(value, axis=0 if system["left"] else 1, keepdims=True)

    for system in systems:
        rhs = system["r"][...]
        system["p"][...] = rhs
        system["x"][...] = jnp.zeros_like(rhs)

    begin = [total(s, s["r"][...] * s["r"][...]) for s in systems]

    def step(carry):
        count, squares, _ = carry
        later, worst = [], jnp.float32(0.0)
        for system, square, first in zip(systems, squares, begin):
            direction = system["p"][...]
            image = times(system, direction)
            curve = total(system, direction * image)
            size = jnp.where(curve > 0.0, square / jnp.where(curve > 0.0, curve, 1.0), 0.0)
            system["x"][...] += size * direction
            rest = system["r"][...] - size * image
            system["r"][...] = rest
            fresh = total(system, rest * rest)
            turn = jnp.where(square > 0.0, fresh / jnp.where(square > 0.0, square, 1.0), 0.0)
            system["p"][...] = rest + turn * direction
            later.append(fresh)
            worst = jnp.maximum(worst, jnp.max(fresh - TOLERANCE * TOLERANCE * first))
        return count + 1, tuple(later), worst

    lax.while_loop(
        lambda carry: jnp.logical_and(carry[0] < MAX_STEPS, carry[2] > 0.0),
        step,
        (jnp.int32(0), tuple(begin), jnp.float32(1.0)),
    )


def eye(size):
    rows = lax.broadcasted_iota(jnp.int32, (size, size), 0)
    cols = lax.broadcasted_iota(jnp.int32, (size, size), 1)
    return jnp.where(rows == cols, 1.0, 0.0).astype(jnp.float32)


def solve_kernel(
    rows_one, rows_two, in_two_ref, grad_two_ref, small_ref, one_ref, two_ref,
    ah1, al1, ah2, al2, bh1, bl1, bh2, bl2, r1, p1, x1, r2, p2, x2,
):
    def put(high_ref, low_ref, value):
        high_ref[...], low_ref[...] = halves(value)

    put(ah1, al1, small_ref[0:128] * (1.0 / rows_one) + damp_input * eye(128))
    put(bh1, bl1, small_ref[160:192, 0:32] * (1.0 / rows_one) + damp_grad * eye(32))
    put(bh2, bl2, small_ref[192:256, 0:64] * (1.0 / rows_two) + damp_grad * eye(64))
    put(ah2, al2, in_two_ref[...] * (1.0 / rows_two) + damp_input * eye(in_two_ref.shape[0]))
    mean_one = small_ref[128:160] * (1.0 / rows_one)
    mean_two = grad_two_ref[...] * (1.0 / rows_two)
    r1[...] = mean_one
    r2[...] = mean_two
    conjugate_gradients([
        dict(high=ah2, low=al2, r=r2, p=p2, x=x2, left=False),
        dict(high=ah1, low=al1, r=r1, p=p1, x=x1, left=False),
    ])
    r1[...] = x1[...]
    r2[...] = x2[...]
    conjugate_gradients([
        dict(high=bh2, low=bl2, r=r2, p=p2, x=x2, left=True),
        dict(high=bh1, low=bl1, r=r1, p=p1, x=x1, left=True),
    ])
    form = jnp.sum(x1[...] * mean_one) + jnp.sum(x2[...] * mean_two)
    entries = 32 * 108 + 64 * 864
    factor = jnp.sqrt(jnp.full((1, 1), entries, jnp.float32) / form)
    one_ref[...] = factor * x1[...]
    two_ref[...] = factor * x2[...]


def passed_along(value, axis, steps):
    count = lax.axis_size(axis)
    leading, last = (max(0, -steps), min(count, count - steps))
    return lax.ppermute(value, axis, [(source, source + steps) for source in range(leading, last)])


def f32(*shape):
    return jax.ShapeDtypeStruct(shape, jnp.float32)


def bf16(*shape):
    return jax.ShapeDtypeStruct(shape, jnp.bfloat16)


def to_phases(volume):
    parts = volume.reshape(4, volume.shape[1] // 4, 4, 8, 4, 8, 4)
    return parts.transpose(2, 4, 6, 0, 1, 3, 5).reshape(256, -1)


def on_device(volume, cotangent, conv_one, conv_two):
    local = volume[0]
    cot = cotangent[0]
    halo = passed_along(local[:, 4:], "space", 1)
    cot_halo = passed_along(cot[:, :PLANE], "space", -1)
    vol = jnp.concatenate([jnp.zeros((256, PLANE), jnp.bfloat16), to_phases(halo), to_phases(local)], axis=1)
    cot_ext = jnp.concatenate([cot, cot_halo, jnp.zeros((64, PLANE), jnp.bfloat16)], axis=1)
    w1 = jnp.pad(conv_one.reshape(32, 108), ((0, 0), (0, 20)))
    taps_two = conv_two.reshape(64, 32, 27)
    w2 = taps_two.transpose(0, 2, 1).reshape(64, 864)
    w2t = taps_two.transpose(2, 1, 0).reshape(864, 64)
    sel = jnp.asarray(selection(), jnp.bfloat16)
    out_two, e1, in_two, grad_two, small = pl.pallas_call(
        local_kernel,
        out_shape=(bf16(64, CELLS), bf16(256, CELLS), f32(864, 864), f32(64, 864), f32(256, 128)),
        scratch_shapes=[
            pltpu.VMEM((SUBROWS, 256), jnp.bfloat16),
            pltpu.VMEM((1024, 256), jnp.bfloat16),
            pltpu.VMEM((864, CELLS), jnp.bfloat16),
        ],
    )(vol, cot_ext, sel, w1, w2, w2t)
    grad_pre = e1.reshape(2, 2, 2, 32, 2, 8, 8).transpose(3, 4, 0, 5, 1, 6, 2).reshape(32, 1024)

    in_two, grad_two, small = lax.psum((in_two, grad_two, small), ("dp", "space"))
    devices = lax.axis_size("dp") * lax.axis_size("space")
    one, two = pl.pallas_call(
        lambda *refs: solve_kernel(1024 * devices, CELLS * devices, *refs),
        out_shape=(f32(32, 128), f32(64, 864)),
        scratch_shapes=[
            pltpu.VMEM((n, n), jnp.bfloat16) for n in (128, 128, 864, 864, 32, 32, 64, 64)
        ]
        + [pltpu.VMEM((32, 128), jnp.float32)] * 3
        + [pltpu.VMEM((64, 864), jnp.float32)] * 3,
    )(in_two, grad_two, small)
    update_one = one[:, :108].reshape(-1)
    update_two = two.reshape(64, 27, 32).transpose(0, 2, 1).reshape(-1)
    return (out_two[None], grad_pre[None], update_one, update_two)


def solution(mesh):
    in_specs = (P("dp", None, "space", None, None), P("dp", None, "space"), P(), P())
    out_specs = (P("dp", None, "space"), P("dp", None, "space"), P(), P())
    return jax.shard_map(
        on_device, mesh=mesh, in_specs=in_specs, out_specs=out_specs, check_vma=False
    )
```

time: 946 us -> 248 us (0.26); the launches traced: 934 us -> 250 us
  other arithmetic: 507 us -> 1.39 us
  local copies, waits for them, and re-layouts: 157 us -> 27.2 us
  Pallas kernels: 0 us -> 62.2 us
  waiting for transfers between devices: 202 us -> 141 us
  matrix products: 37.8 us -> 0 us
    another operation x49 -> x0, other arithmetic: 258 us -> none  [the longest x36 166 us: damped_solve(): lower_factor = jnp.linalg.cholesky(matrix)]
    scatter-add x28 -> x0, other arithmetic: 236 us -> none  [the longest x27 235 us: spread_taps(): canvas = canvas.at[:, depth_tap:depth_tap + 2 * out_depth:2, row_tap:row_...]
    slice x57 -> x1, local copies, waits for them, and re-layouts: 91.1 us -> 0.92 us  [on_device(): halo = passed_along(local[:, 4:], 'space', 1)]
    pallas_call x0 -> x2, Pallas kernels: none -> 62.2 us  [the longest x1 55.9 us: on_device(): pl.pallas_call(lambda *refs: solve_kernel(1024 * devices, CELLS * devices...]
    psum x2 -> x1, waiting for transfers between devices: 202 us -> 141 us  [on_device(): lax.psum((in_two, grad_two, small), ('dp', 'space'))]
    another operation x44 -> x0, matrix products: 30 us -> none  [the longest x32 17.9 us: damped_solve(): return jax.scipy.linalg.cho_solve((lower_factor, True), rhs_terms)]
    unnamed x95 -> x6, local copies, waits for them, and re-layouts: 27 us -> 2.34 us
    another operation x34 -> x1, local copies, waits for them, and re-layouts: 25.7 us -> 2.56 us  [to_phases(): parts = volume.reshape(4, volume.shape[1] // 4, 4, 8, 4, 8, 4)]
  transfers between devices with their start and end apart: 5 -> 3, of which waited for: 2 -> 1; matrix products, arithmetic and copies ran while one was open for 19% -> 7% of each run, Pallas kernels for 0% -> 0%
where the time goes in v1:
time: 248 us; the launch traced here: 250 us
  waiting for transfers between devices  141 us (57%)
  Pallas kernels  62.2 us (25%)
  local copies, waits for them, and re-layouts  27.2 us (11%)
  between operations  14.1 us (6%)
  starting transfers between devices  4.37 us (2%)
    psum x1, waiting for transfers between devices, on_device(): lax.psum((in_two, grad_two, small), ('dp', 'space'))  141 us
    pallas_call x1, Pallas kernels, on_device(): pl.pallas_call(lambda *refs: solve_kernel(1024 * devices, CELLS * devices...  55.9 us
    transpose x2, local copies, waits for them, and re-layouts, to_phases(): return parts.transpose(2, 4, 6, 0, 1, 3, 5).reshape(256, -1)  11.3 us
    pallas_call x1, Pallas kernels, on_device(): pl.pallas_call(local_kernel, out_shape=(bf16(64, CELLS), bf16(256, CELLS)...  6.31 us
  transfers between devices with their start and end apart: 3, of which 1 were waited for; matrix products, arithmetic and copies ran while one was open for 7% of the time, Pallas kernels for 0%

profile of v1, /device:TPU:0, one launch (start us, length us, event | category | flops | bytes accessed | tf_op | source)
XLA Modules:
  0.0 250.3 jit_solution(15082924313861588925)
XLA Ops:
  7.2 1.3 collective-permute-start.1
  8.5 0.9 slice.12
  9.4 3.0 %collective-permute-start = (bf16[4,4,32,32]{3,2,1,0:T(8,128)(2,1)S(1)}, bf16[4,4,32,32]{3,2,1,0:T(8,128)(2,1)S(1)}, u32[]{:S(2)}, u32[]{:S(2)}) collective-permute-start(bf16[4,4,32,32]{3,2,1,0:T(8,128)(2,1)S(1)} %slice.12), channel_id=1, source_target_pairs={{0,1},{1,2},{2,3},{4,5},{5,6},{6,7},{8,9},{9,10},{10,11},{12,13},{... | collective-permute-start | bytes 98312 | tf_op jit(solution)/shard_map/ppermute | solution.py:242
  12.6 2.6 %reshape_squeeze.3 = bf16[4,2,4,8,4,8,4]{6,5,4,3,2,1,0:T(8,128)(2,1)S(1)} reshape(bf16[1,4,8,32,32]{4,3,2,1,0:T(8,128)(2,1)} %param.5) | data formatting | bytes 131072 | tf_op jit(solution)/shard_map/reshape;squeeze | solution.py:254
  15.1 0.8 copy.16
  16.0 0.6 pad.4.w1_ref
  16.6 1.7 copy.18.w2_ref
  18.4 7.6 %copy.15 = bf16[4,4,4,4,2,8,8]{6,5,4,3,2,1,0:T(8,128)(2,1)S(1)} copy(bf16[4,4,4,4,2,8,8]{2,6,1,5,0,4,3:T(8,128)(2,1)S(1)} %bitcast.35) | data formatting | bytes 131072 | tf_op jit(solution)/shard_map/transpose | solution.py:255
  26.0 1.1 reshape.43
  27.1 0.6 maximum_maximum_fusion.c_ref
  27.7 0.7 reshape.41
  28.4 3.7 %copy.14 = bf16[4,4,4,4,1,8,8]{6,5,3,2,1,0,4:T(8,128)(2,1)S(1)} copy(bf16[4,4,4,4,1,8,8]{2,6,1,5,0,3,4:T(8,128)(2,1)S(1)} %bitcast.36) | data formatting | bytes 65536 | tf_op jit(solution)/shard_map/transpose | solution.py:255
  32.1 0.3 reshape.42
  32.4 0.8 pad_maximum_fusion.v_ref
  33.2 6.3 %shard_map.84 = (bf16[64,128]{1,0:T(8,128)(2,1)}, bf16[256,128]{1,0:T(8,128)(2,1)}, f32[864,864]{1,0:T(8,128)}, f32[64,864]{1,0:T(8,128)}, f32[256,128]{1,0:T(8,128)}) custom-call(bf16[256,256]{1,0:T(8,128)(2,1)} %pad_maximum_fusion.v_ref, bf16[64,256]{1,0:T(8,128)(2,1)} %maximum_maximum_fusion.c_ref, bf16[1024,896]{1,0:T(8,128)(2,1)} %constant.3.clone.sel_ref, ...), custom_call_target="tpu_custom_call" | custom-call | tf_op jit(solution)/shard_map/pallas_call | solution.py:270
  39.5 0.8 copy-done
  40.6 0.2 copy.20
  40.8 0.8 copy.23
  41.6 141.0 %all-reduce.4.cloned.1.call-done = (f32[864,864]{1,0:T(8,128)}, f32[64,864]{1,0:T(8,128)}, f32[256,128]{1,0:T(8,128)}) async-done(((f32[864,864]{1,0:T(8,128)}, f32[64,864]{1,0:T(8,128)}, f32[256,128]{1,0:T(8,128)}), (f32[864,864]{1,0:T(8,128)}, f32[64,864]{1,0:T(8,128)}, f32[256,128]{1,0:T(8,128)})) %all-reduce.4.cloned.1.call-update) | async-done | bytes 3338256 | tf_op jit(solution)/shard_map/psum | solution.py:281
  182.5 55.9 %shard_map.85 = (f32[32,128]{1,0:T(8,128)}, f32[64,864]{1,0:T(8,128)}) custom-call(f32[864,864]{1,0:T(8,128)} %get-tuple-element.22.refs_0_, f32[64,864]{1,0:T(8,128)} %get-tuple-element.23.refs_1_, f32[256,128]{1,0:T(8,128)} %get-tuple-element.24.refs_2_), custom_call_target="tpu_custom_call" | custom-call | tf_op jit(solution)/shard_map/pallas_call | solution.py:283
  238.4 1.4 reshape.49
  239.8 1.1 copy.21
  241.0 1.0 copy.22
  242.0 1.5 reshape.51
  (13 shorter events, 0.5 us)
Async XLA Ops:
  7.2 175.4 %all-reduce.4.cloned.1.call-start = ((), (), s32[]{:S(2)}) async-start(), calls=%async_computation | async-start | bytes 6914048 | tf_op jit(solution)/shard_map/psum | solution.py:281
  7.2 19.9 %collective-permute-start.1 = (bf16[64,64]{1,0:T(8,128)(2,1)}, bf16[64,64]{1,0:T(8,128)(2,1)S(1)}, u32[]{:S(2)}, u32[]{:S(2)}) collective-permute-start(bf16[64,64]{1,0:T(8,128)(2,1)} %bitcast.44), channel_id=1, source_target_pairs={{1,0},{2,1},{3,2},{5,4},{6,5},{7,6},{9,8},{10,9},{11,10},{13,12},{... | collective-permute-start | bytes 24584 | tf_op jit(solution)/shard_map/ppermute | solution.py:242
  9.4 18.3 %collective-permute-start = (bf16[4,4,32,32]{3,2,1,0:T(8,128)(2,1)S(1)}, bf16[4,4,32,32]{3,2,1,0:T(8,128)(2,1)S(1)}, u32[]{:S(2)}, u32[]{:S(2)}) collective-permute-start(bf16[4,4,32,32]{3,2,1,0:T(8,128)(2,1)S(1)} %slice.12), channel_id=1, source_target_pairs={{0,1},{1,2},{2,3},{4,5},{5,6},{6,7},{8,9},{9,10},{10,11},{12,13},{... | collective-permute-start | bytes 98312 | tf_op jit(solution)/shard_map/ppermute | solution.py:242
  12.6 14.5 %copy-start.1 = (bf16[1,64,128]{2,1,0:T(8,128)(2,1)S(1)}, bf16[1,64,128]{2,1,0:T(8,128)(2,1)}, u32[]{:S(2)}) copy-start(bf16[1,64,128]{2,1,0:T(8,128)(2,1)} %param.6) | copy-start | bytes 49156
  39.5 0.8 copy-start
Sparse Core Ops, SparseCore 0:
  39.6 142.8 all-reduce.3

commit v2 on v1

--- a/solution.py
+++ b/solution.py
@@ -16,6 +16,9 @@
 TAPS = [(a, b, e) for a in range(3) for b in range(3) for e in range(3)]
 PHASES = [(d, h, w) for d in (0, 1) for h in (0, 1) for w in (0, 1)]
 SUBROWS = 896
+HALF = 160
+SUMS = 192
+GROUP = 4
 
 
 def block_rows():
@@ -68,7 +71,7 @@
 
 def local_kernel(
     v_ref, c_ref, sel_ref, w1_ref, w2_ref, w2t_ref,
-    out_ref, e1_ref, in_two_ref, grad_two_ref, small_ref,
+    out_ref, e1_ref, a_ref, b_ref, small_ref,
     x_ref, p1_ref, p2_ref,
 ):
     lane = lax.broadcasted_iota(jnp.int32, (256, 256), 1)
@@ -98,7 +101,11 @@
     pre = [dot(w1_ref[...], p1_ref[ph * 128 : ph * 128 + 128]) for ph in range(8)]
     pre = jnp.concatenate(pre, axis=0)
     sig = 1.0 / (1.0 + jnp.exp(-pre))
-    act = (pre * sig).astype(jnp.bfloat16).astype(jnp.float32)
+    act = (pre * sig).astype(jnp.bfloat16)
+    a_ref[...] = act[:HALF, CELLS:]
+    b_ref[0 : 256 - HALF] = act[HALF:, CELLS:]
+    b_ref[256 - HALF :] = c_ref[:, :CELLS]
+    act = act.astype(jnp.float32)
 
     p_own, q_own = p_all[:32, :CELLS], q_all[:32, :CELLS]
     for t, tap in enumerate(TAPS):
@@ -136,14 +143,89 @@
         in_one += dot_t(p1, p1)
         grad_one += dot_t(piece, p1)
         gram_one += dot_t(piece, piece)
-    own_cot = c_ref[:, :CELLS]
-    small_ref[...] = jnp.zeros((256, 128), jnp.float32)
+    small_ref[...] = jnp.zeros((SUMS, 128), jnp.float32)
     small_ref[0:128] = in_one
     small_ref[128:160] = grad_one
     small_ref[160:192, 0:32] = gram_one
-    small_ref[192:256, 0:64] = dot_t(own_cot, own_cot)
-    grad_two_ref[...] = dot_t(own_cot, p2)
-    in_two_ref[...] = dot_t(p2, p2)
+
+
+def coordinates():
+    return {"dp": lax.axis_index("dp"), "space": lax.axis_index("space")}
+
+
+def bit_of(value, bit):
+    return (value // 2**bit) % 2
+
+
+def position(order, coords):
+    return sum(bit_of(coords[axis], bit) * 2**stage for stage, (axis, bit) in enumerate(order))
+
+
+def orders(count_dp, count_space):
+    dp_bits = [("dp", bit) for bit in reversed(range(count_dp.bit_length() - 1))]
+    space_bits = [("space", bit) for bit in reversed(range(count_space.bit_length() - 1))]
+    first = dp_bits + space_bits
+    second = space_bits[:-1] + dp_bits + space_bits[-1:]
+    sums = space_bits[-1:] + dp_bits[::-1] + space_bits[:-1]
+    return first, second, sums
+
+
+def exchange_kernel(
+    plan, a_ref, b_ref, small_ref, ga_ref, gb_ref, total_ref, run_ref, land_ref,
+    own_sem, send_sem, recv_sem,
+):
+    order_a, order_b, order_s = plan
+    coords = coordinates()
+    stages = len(order_a)
+
+    def partner(axis, bit):
+        at = coords[axis]
+        other = at + (1 - 2 * bit_of(at, bit)) * 2**bit
+        return {axis: other}
+
+    barrier = pltpu.get_barrier_semaphore()
+    for axis, bit in order_a:
+        pl.semaphore_signal(
+            barrier, inc=1, device_id=partner(axis, bit), device_id_type=pl.DeviceIdType.MESH
+        )
+    spots = [position(order_a, coords), position(order_b, coords)]
+    owns = []
+    for k, (src, dst) in enumerate(((a_ref, ga_ref), (b_ref, gb_ref))):
+        own = pltpu.make_async_copy(src, dst.at[spots[k]], own_sem.at[k])
+        own.start()
+        owns.append(own)
+    for own in owns:
+        own.wait()
+    pl.semaphore_wait(barrier, stages)
+
+    for stage in range(stages):
+        copies = []
+        for k, (order, ref) in enumerate(((order_a, ga_ref), (order_b, gb_ref))):
+            base = (spots[k] // 2**stage) * 2**stage
+            held = ref.at[pl.ds(base, 2**stage)]
+            copies.append((k, order[stage], held, held))
+        source = small_ref if stage == 0 else run_ref.at[stage - 1]
+        copies.append((2, order_s[stage], source, land_ref.at[stage]))
+        sent = []
+        for k, (axis, bit), src, dst in copies:
+            copy = pltpu.make_async_remote_copy(
+                src_ref=src,
+                dst_ref=dst,
+                send_sem=send_sem.at[stage, k],
+                recv_sem=recv_sem.at[stage, k],
+                device_id=partner(axis, bit),
+                device_id_type=pl.DeviceIdType.MESH,
+            )
+            copy.start()
+            sent.append(copy)
+        sent[2].wait()
+        running = (small_ref[...] if stage == 0 else run_ref[stage - 1]) + land_ref[stage]
+        if stage < stages - 1:
+            run_ref[stage] = running
+        else:
+            total_ref[...] = running
+        sent[0].wait()
+        sent[1].wait()
 
 
 def halves(value):
@@ -204,19 +286,77 @@
     return jnp.where(rows == cols, 1.0, 0.0).astype(jnp.float32)
 
 
+def slab_patches(act, below, out_ref, column):
+    lane = lax.broadcasted_iota(jnp.int32, (128, CELLS), 1)
+    act = act.astype(jnp.float32)
+    odd = act[128:]
+    shifted = pltpu.roll(jnp.where(lane >= PLANE, below.astype(jnp.float32), odd), PLANE, 1)
+    row0 = (lane[:32] // 8) % 8 == 0
+    col0 = lane[:32] % 8 == 0
+    for a, base in ((0, shifted), (1, act[:128]), (2, odd)):
+        for b in range(3):
+            for e in range(3):
+                start = 64 * (b != 1) + 32 * (e != 1)
+                rows = base[start : start + 32]
+                shift = 8 * (b == 0) + (e == 0)
+                if shift:
+                    rows = pltpu.roll(rows, shift, 1)
+                if b == 0:
+                    rows = jnp.where(row0, 0.0, rows)
+                if e == 0:
+                    rows = jnp.where(col0, 0.0, rows)
+                t = 9 * a + 3 * b + e
+                out_ref[t * 32 : t * 32 + 32, column : column + CELLS] = rows.astype(jnp.bfloat16)
+
+
 def solve_kernel(
-    rows_one, rows_two, in_two_ref, grad_two_ref, small_ref, one_ref, two_ref,
-    ah1, al1, ah2, al2, bh1, bl1, bh2, bl2, r1, p1, x1, r2, p2, x2,
+    plan, counts, ga_ref, gb_ref, small_ref, one_ref, two_ref,
+    ah1, al1, ah2, al2, bh1, bl1, bh2, bl2, r1, p1, x1, r2, p2, x2, cols_ref, in_two_ref, side_ref,
 ):
+    count_dp, count_space = counts
+    devices = count_dp * count_space
+    rows_one, rows_two = 8 * CELLS * devices, CELLS * devices
+    group = min(GROUP, count_space)
+
+    def slab(dp, space):
+        coords = {"dp": dp, "space": space}
+        return ga_ref[position(plan[0], coords)], gb_ref[position(plan[1], coords)]
+
+    def gather_group(index):
+        dp, first = index % count_dp, (index // count_dp) * group
+        for k in range(group):
+            low, high = slab(dp, first + k)
+            if k > 0:
+                below = before
+            else:
+                a, b = slab(dp, jnp.maximum(first - 1, 0))
+                below = jnp.concatenate([a[128:], b[: 256 - HALF]], axis=0)
+                below = jnp.where(first > 0, below, jnp.zeros_like(below))
+            act = jnp.concatenate([low, high[: 256 - HALF]], axis=0)
+            before = act[128:]
+            slab_patches(act, below, cols_ref, k * CELLS)
+            cols_ref[864:, k * CELLS : (k + 1) * CELLS] = high[256 - HALF :]
+
+    in_two_ref[...] = jnp.zeros_like(in_two_ref)
+    side_ref[...] = jnp.zeros_like(side_ref)
+
+    def accumulate(index, carry):
+        gather_group(index)
+        in_two_ref[...] += dot_t(cols_ref[:864], cols_ref[:864])
+        side_ref[...] += dot_t(cols_ref[864:], cols_ref[...])
+        return carry
+
+    lax.fori_loop(0, devices // group, accumulate, 0)
+
     def put(high_ref, low_ref, value):
         high_ref[...], low_ref[...] = halves(value)
 
     put(ah1, al1, small_ref[0:128] * (1.0 / rows_one) + damp_input * eye(128))
     put(bh1, bl1, small_ref[160:192, 0:32] * (1.0 / rows_one) + damp_grad * eye(32))
-    put(bh2, bl2, small_ref[192:256, 0:64] * (1.0 / rows_two) + damp_grad * eye(64))
+    put(bh2, bl2, side_ref[:, 864:] * (1.0 / rows_two) + damp_grad * eye(64))
     put(ah2, al2, in_two_ref[...] * (1.0 / rows_two) + damp_input * eye(in_two_ref.shape[0]))
     mean_one = small_ref[128:160] * (1.0 / rows_one)
-    mean_two = grad_two_ref[...] * (1.0 / rows_two)
+    mean_two = side_ref[:, :864] * (1.0 / rows_two)
     r1[...] = mean_one
     r2[...] = mean_two
     conjugate_gradients([
@@ -258,18 +398,19 @@
 def on_device(volume, cotangent, conv_one, conv_two):
     local = volume[0]
     cot = cotangent[0]
-    halo = passed_along(local[:, 4:], "space", 1)
+    phases = to_phases(local)
+    halo = passed_along(phases[:, PLANE:], "space", 1)
     cot_halo = passed_along(cot[:, :PLANE], "space", -1)
-    vol = jnp.concatenate([jnp.zeros((256, PLANE), jnp.bfloat16), to_phases(halo), to_phases(local)], axis=1)
+    vol = jnp.concatenate([jnp.zeros((256, PLANE), jnp.bfloat16), halo, phases], axis=1)
     cot_ext = jnp.concatenate([cot, cot_halo, jnp.zeros((64, PLANE), jnp.bfloat16)], axis=1)
     w1 = jnp.pad(conv_one.reshape(32, 108), ((0, 0), (0, 20)))
     taps_two = conv_two.reshape(64, 32, 27)
     w2 = taps_two.transpose(0, 2, 1).reshape(64, 864)
     w2t = taps_two.transpose(2, 1, 0).reshape(864, 64)
     sel = jnp.asarray(selection(), jnp.bfloat16)
-    out_two, e1, in_two, grad_two, small = pl.pallas_call(
+    out_two, e1, block_a, block_b, small = pl.pallas_call(
         local_kernel,
-        out_shape=(bf16(64, CELLS), bf16(256, CELLS), f32(864, 864), f32(64, 864), f32(256, 128)),
+        out_shape=(bf16(64, CELLS), bf16(256, CELLS), bf16(HALF, CELLS), bf16(320 - HALF, CELLS), f32(SUMS, 128)),
         scratch_shapes=[
             pltpu.VMEM((SUBROWS, 256), jnp.bfloat16),
             pltpu.VMEM((1024, 256), jnp.bfloat16),
@@ -278,17 +419,38 @@
     )(vol, cot_ext, sel, w1, w2, w2t)
     grad_pre = e1.reshape(2, 2, 2, 32, 2, 8, 8).transpose(3, 4, 0, 5, 1, 6, 2).reshape(32, 1024)
 
-    in_two, grad_two, small = lax.psum((in_two, grad_two, small), ("dp", "space"))
-    devices = lax.axis_size("dp") * lax.axis_size("space")
+    counts = (lax.axis_size("dp"), lax.axis_size("space"))
+    plan = orders(*counts)
+    stages = len(plan[0])
+    devices = counts[0] * counts[1]
+    all_a, all_b, small = pl.pallas_call(
+        lambda *refs: exchange_kernel(plan, *refs),
+        out_shape=(bf16(devices, HALF, CELLS), bf16(devices, 320 - HALF, CELLS), f32(SUMS, 128)),
+        in_specs=[pl.BlockSpec(memory_space=pltpu.VMEM)] * 3,
+        out_specs=[pl.BlockSpec(memory_space=pltpu.VMEM)] * 3,
+        scratch_shapes=[
+            pltpu.VMEM((stages, SUMS, 128), jnp.float32),
+            pltpu.VMEM((stages, SUMS, 128), jnp.float32),
+            pltpu.SemaphoreType.DMA((2,)),
+            pltpu.SemaphoreType.DMA((stages, 3)),
+            pltpu.SemaphoreType.DMA((stages, 3)),
+        ],
+        compiler_params=pltpu.CompilerParams(collective_id=0, has_side_effects=True),
+    )(block_a, block_b, small)
     one, two = pl.pallas_call(
-        lambda *refs: solve_kernel(1024 * devices, CELLS * devices, *refs),
+        lambda *refs: solve_kernel(plan, counts, *refs),
         out_shape=(f32(32, 128), f32(64, 864)),
         scratch_shapes=[
             pltpu.VMEM((n, n), jnp.bfloat16) for n in (128, 128, 864, 864, 32, 32, 64, 64)
         ]
         + [pltpu.VMEM((32, 128), jnp.float32)] * 3
-        + [pltpu.VMEM((64, 864), jnp.float32)] * 3,
-    )(in_two, grad_two, small)
+        + [pltpu.VMEM((64, 864), jnp.float32)] * 3
+        + [
+            pltpu.VMEM((928, min(GROUP, counts[1]) * CELLS), jnp.bfloat16),
+            pltpu.VMEM((864, 864), jnp.float32),
+            pltpu.VMEM((64, 928), jnp.float32),
+        ],
+    )(all_a, all_b, small)
     update_one = one[:, :108].reshape(-1)
     update_two = two.reshape(64, 27, 32).transpose(0, 2, 1).reshape(-1)
     return (out_two[None], grad_pre[None], update_one, update_two)

time: 248 us -> 131 us (0.53)
  waiting for transfers between devices: 141 us -> 2.07 us
  Pallas kernels: 62.2 us -> 106 us
  between operations: 14.1 us -> 0.76 us
  local copies, waits for them, and re-layouts: 27.2 us -> 18.5 us
    psum x1 -> x0, waiting for transfers between devices: 141 us -> none  [on_device(): lax.psum((in_two, grad_two, small), ('dp', 'space'))]
    pallas_call x1 -> x2, Pallas kernels: 55.9 us -> 101 us  [the longest x1 65.4 us: on_device(): pl.pallas_call(lambda *refs: solve_kernel(plan, counts, *refs), out_shape...]
    transpose x2 -> x1, local copies, waits for them, and re-layouts: 11.3 us -> 7.65 us  [to_phases(): return parts.transpose(2, 4, 6, 0, 1, 3, 5).reshape(256, -1)]
  transfers between devices with their start and end apart: 3 -> 2, of which waited for: 1 -> 1; matrix products, arithmetic and copies ran while one was open for 7% -> 2% of each run, Pallas kernels for 0% -> 0%
where the time goes in v2:
time: 131 us; the launch traced here: 132 us
  Pallas kernels  106 us (81%)
  local copies, waits for them, and re-layouts  18.5 us (14%)
  starting transfers between devices  3.87 us (3%)
  waiting for transfers between devices  2.07 us (2%)
  other arithmetic  1.38 us (1%)
    pallas_call x1, Pallas kernels, on_device(): pl.pallas_call(lambda *refs: solve_kernel(plan, counts, *refs), out_shape...  65.4 us
    pallas_call x1, Pallas kernels, on_device(): pl.pallas_call(lambda *refs: exchange_kernel(plan, *refs), out_shape=(bf1...  35.7 us
    transpose x1, local copies, waits for them, and re-layouts, to_phases(): return parts.transpose(2, 4, 6, 0, 1, 3, 5).reshape(256, -1)  7.65 us
    pallas_call x1, Pallas kernels, on_device(): pl.pallas_call(local_kernel, out_shape=(bf16(64, CELLS), bf16(256, CELLS)...  4.74 us
    ppermute x2, starting transfers between devices, passed_along(): lax.ppermute(value, axis, [(source, source + steps) for source in range(l...  3.87 us
  transfers between devices with their start and end apart: 2, of which 1 were waited for; matrix products, arithmetic and copies ran while one was open for 2% of the time, Pallas kernels for 0%

profile of v2, /device:TPU:0, one launch (start us, length us, event | category | flops | bytes accessed | tf_op | source)
XLA Modules:
  0.0 132.5 jit_solution(1882433319762817664)
XLA Ops:
  0.6 2.6 %reshape_squeeze.3 = bf16[4,2,4,8,4,8,4]{6,5,4,3,2,1,0:T(8,128)(2,1)S(1)} reshape(bf16[1,4,8,32,32]{4,3,2,1,0:T(8,128)(2,1)} %param.5) | data formatting | bytes 131072 | tf_op jit(solution)/shard_map/reshape;squeeze | solution.py:394
  3.2 7.7 %copy.13 = bf16[4,4,4,4,2,8,8]{6,5,4,3,2,1,0:T(8,128)(2,1)S(1)} copy(bf16[4,4,4,4,2,8,8]{2,6,1,5,0,4,3:T(8,128)(2,1)S(1)} %bitcast.27) | data formatting | bytes 131072 | tf_op jit(solution)/shard_map/transpose | solution.py:395
  10.9 1.1 reshape.35
  12.0 0.1 slice.12
  12.1 2.4 %collective-permute-start = (bf16[256,64]{1,0:T(8,128)(2,1)S(1)}, bf16[256,64]{1,0:T(8,128)(2,1)S(1)}, u32[]{:S(2)}, u32[]{:S(2)}) collective-permute-start(bf16[256,64]{1,0:T(8,128)(2,1)S(1)} %slice.12), channel_id=1, source_target_pairs={{0,1},{1,2},{2,3},{4,5},{5,6},{6,7},{8,9},{9,10},{10,11},{12,13},{... | collective-permute-start | bytes 98312 | tf_op jit(solution)/shard_map/ppermute | solution.py:382
  14.5 1.5 %collective-permute-start.1 = (bf16[64,64]{1,0:T(8,128)(2,1)S(1)}, bf16[64,64]{1,0:T(8,128)(2,1)S(1)}, u32[]{:S(2)}, u32[]{:S(2)}) collective-permute-start(bf16[64,64]{1,0:T(8,128)(2,1)S(1)} %bitcast.34), channel_id=1, source_target_pairs={{1,0},{2,1},{3,2},{5,4},{6,5},{7,6},{9,8},{10,9},{11,10},{13,12},{... | collective-permute-start | bytes 24584 | tf_op jit(solution)/shard_map/ppermute | solution.py:382
  16.0 0.1 fusion
  16.0 0.8 copy.16.w2_ref
  16.9 0.1 copy.15
  16.9 0.6 pad.4.w1_ref
  17.6 2.1 %collective-permute-done.1 = bf16[64,64]{1,0:T(8,128)(2,1)S(1)} collective-permute-done((bf16[64,64]{1,0:T(8,128)(2,1)S(1)}, bf16[64,64]{1,0:T(8,128)(2,1)S(1)}, u32[]{:S(2)}, u32[]{:S(2)}) %collective-permute-start.1) | collective-permute-done | bytes 8224 | tf_op jit(solution)/shard_map/ppermute | solution.py:382
  19.6 0.6 maximum_maximum_fusion.c_ref
  20.3 0.8 pad_maximum_fusion.v_ref
  21.0 4.7 %shard_map.84 = (bf16[64,128]{1,0:T(8,128)(2,1)}, bf16[256,128]{1,0:T(8,128)(2,1)}, bf16[160,128]{1,0:T(8,128)(2,1)}, bf16[160,128]{1,0:T(8,128)(2,1)}, f32[192,128]{1,0:T(8,128)}) custom-call(bf16[256,256]{1,0:T(8,128)(2,1)} %pad_maximum_fusion.v_ref, bf16[64,256]{1,0:T(8,128)(2,1)} %maximum_maximum_fusion.c_ref, bf16[1024,896]{1,0:T(8,128)(2,1)} %constant.3.clone.sel_ref, ...), custom_call_target="tpu_custom_call" | custom-call | tf_op jit(solution)/shard_map/pallas_call | solution.py:411
  25.8 35.7 %shard_map.85 = (bf16[32,160,128]{2,1,0:T(8,128)(2,1)}, bf16[32,160,128]{2,1,0:T(8,128)(2,1)}, f32[192,128]{1,0:T(8,128)}) custom-call(bf16[160,128]{1,0:T(8,128)(2,1)} %get-tuple-element.16.refs_0_, bf16[160,128]{1,0:T(8,128)(2,1)} %get-tuple-element.17.refs_1_, f32[192,128]{1,0:T(8,128)} %get-tuple-element.18.refs_2_), custom_call_target="tpu_custom_call" | custom-call | tf_op jit(solution)/shard_map/pallas_call | solution.py:426
  61.4 65.4 %shard_map.86 = (f32[32,128]{1,0:T(8,128)}, f32[64,864]{1,0:T(8,128)}) custom-call(bf16[32,160,128]{2,1,0:T(8,128)(2,1)} %get-tuple-element.19.refs_0_, bf16[32,160,128]{2,1,0:T(8,128)(2,1)} %get-tuple-element.20.refs_1_, f32[192,128]{1,0:T(8,128)} %get-tuple-element.21.refs_2_), custom_call_target="tpu_custom_call" | custom-call | tf_op jit(solution)/shard_map/pallas_call | solution.py:440
  126.9 1.2 copy.19
  128.1 1.0 copy.20
  129.1 1.5 %reshape.43 = f32[55296]{0:T(1024)} reshape(f32[64,32,27]{2,1,0:T(8,128)S(1)} %copy.20) | data formatting | bytes 442368 | tf_op jit(solution)/shard_map/reshape | solution.py:455
  130.5 0.7 reshape.41
  131.2 0.1 copy.17
  131.3 0.2 reshape.40
  131.5 0.2 copy.18
  131.7 0.8 copy.21
  (14 shorter events, 0.1 us)
Async XLA Ops:
  3.2 11.3 %copy-start.4 = (bf16[1,64,128]{2,1,0:T(8,128)(2,1)S(1)}, bf16[1,64,128]{2,1,0:T(8,128)(2,1)}, u32[]{:S(2)}) copy-start(bf16[1,64,128]{2,1,0:T(8,128)(2,1)} %param.6) | copy-start | bytes 49156
  3.2 12.8 %copy-start = (bf16[64,32,3,3,3]{0,1,4,3,2:T(8,128)(2,1)S(1)}, bf16[64,32,3,3,3]{0,1,4,3,2:T(8,128)(2,1)}, u32[]{:S(2)}) copy-start(bf16[64,32,3,3,3]{0,1,4,3,2:T(8,128)(2,1)} %param.8) | copy-start | bytes 331780
  3.2 13.6 %copy-start.2 = (bf16[32,4,3,3,3]{0,1,4,3,2:T(4,128)(2,1)S(1)}, bf16[32,4,3,3,3]{0,1,4,3,2:T(4,128)(2,1)}, u32[]{:S(2)}) copy-start(bf16[32,4,3,3,3]{0,1,4,3,2:T(4,128)(2,1)} %param.7) | copy-start | bytes 20740
  12.1 8.2 %collective-permute-start = (bf16[256,64]{1,0:T(8,128)(2,1)S(1)}, bf16[256,64]{1,0:T(8,128)(2,1)S(1)}, u32[]{:S(2)}, u32[]{:S(2)}) collective-permute-start(bf16[256,64]{1,0:T(8,128)(2,1)S(1)} %slice.12), channel_id=1, source_target_pairs={{0,1},{1,2},{2,3},{4,5},{5,6},{6,7},{8,9},{9,10},{10,11},{12,13},{... | collective-permute-start | bytes 98312 | tf_op jit(solution)/shard_map/ppermute | solution.py:382
  14.5 5.2 %collective-permute-start.1 = (bf16[64,64]{1,0:T(8,128)(2,1)S(1)}, bf16[64,64]{1,0:T(8,128)(2,1)S(1)}, u32[]{:S(2)}, u32[]{:S(2)}) collective-permute-start(bf16[64,64]{1,0:T(8,128)(2,1)S(1)} %bitcast.34), channel_id=1, source_target_pairs={{1,0},{2,1},{3,2},{5,4},{6,5},{7,6},{9,8},{10,9},{11,10},{13,12},{... | collective-permute-start | bytes 24584 | tf_op jit(solution)/shard_map/ppermute | solution.py:382
  126.9 3.6 %copy-start.3 = (f32[32,128]{1,0:T(8,128)S(1)}, f32[32,128]{1,0:T(8,128)}, u32[]{:S(2)}) copy-start(f32[32,128]{1,0:T(8,128)} %get-tuple-element.22) | copy-start | bytes 49156
  126.9 4.3 %copy-start.1 = (bf16[256,128]{1,0:T(8,128)(2,1)S(1)}, bf16[256,128]{1,0:T(8,128)(2,1)}, u32[]{:S(2)}) copy-start(bf16[256,128]{1,0:T(8,128)(2,1)} %get-tuple-element.15) | copy-start | bytes 196612

commit v3 on v2

--- a/solution.py
+++ b/solution.py
@@ -12,7 +12,7 @@
 MAX_STEPS = 5000
 CELLS = 128
 PLANE = 64
-BLOCKS_ONE = [(sd, sh, sw) for sd in (0, 1) for sh in (0, 1) for sw in (0, 1)]
+SHIFTS = [(sd, sh, sw) for sd in (0, 1) for sh in (0, 1) for sw in (0, 1)]
 TAPS = [(a, b, e) for a in range(3) for b in range(3) for e in range(3)]
 PHASES = [(d, h, w) for d in (0, 1) for h in (0, 1) for w in (0, 1)]
 SUBROWS = 896
@@ -23,14 +23,30 @@
 
 def block_rows():
     table, row = {}, 0
-    for sd, sh, sw in BLOCKS_ONE:
-        for md in (3,) if sd else range(4):
-            for mh in (3,) if sh else range(4):
-                for mw in range(4):
+    for sd, sh, sw in SHIFTS:
+        for mw in (3,) if sw else range(4):
+            for md in (3,) if sd else range(4):
+                for mh in range(4):
                     for c in range(4):
                         table[(sd, sh, sw, md, mh, mw, c)] = row
                         row += 1
     return table
+
+
+def column_spread():
+    spread = np.zeros((32, 4, 16, 8), np.float32)
+    for w in range(32):
+        spread[w, w % 4, :, w // 4] = 1.0
+    return spread.reshape(32, 512)
+
+
+def row_sums(planes):
+    sums = np.zeros((4, 4, 4, 4, planes, 32), np.float32)
+    for c in range(4):
+        for d in range(planes):
+            for h in range(32):
+                sums[d % 4, h % 4, c, c, d, h] = 1.0
+    return sums.reshape(64, -1)
 
 
 def selection():
@@ -69,18 +85,34 @@
     return rows.astype(jnp.bfloat16)
 
 
+def volume_phases(rows, spread, sums, planes, first):
+    wide = dot(rows, spread)
+    row = lax.broadcasted_iota(jnp.int32, wide.shape, 0)
+    lane = lax.broadcasted_iota(jnp.int32, wide.shape, 1)
+    cell = first + (row % (32 * planes)) // 128
+    keep = (lane % 128) // 8 == 8 * cell + (row % 32) // 4
+    phases = dot(sums, jnp.where(keep, wide, 0.0).astype(jnp.bfloat16))
+    return jnp.concatenate([phases[:, mw * 128 : mw * 128 + 128] for mw in range(4)], axis=0)
+
+
 def local_kernel(
-    v_ref, c_ref, sel_ref, w1_ref, w2_ref, w2t_ref,
+    v_ref, halo_ref, spread_ref, sums_ref, halo_sums_ref, c_ref, sel_ref, w1_ref, w2_ref, w2t_ref,
     out_ref, e1_ref, a_ref, b_ref, small_ref,
     x_ref, p1_ref, p2_ref,
 ):
     lane = lax.broadcasted_iota(jnp.int32, (256, 256), 1)
     p_all = (lane // 8) % 8
     q_all = lane % 8
-    vol = v_ref[...].astype(jnp.float32)
+    vol = jnp.concatenate(
+        [
+            volume_phases(halo_ref[...], spread_ref[...], halo_sums_ref[...], 4, 1),
+            volume_phases(v_ref[...], spread_ref[...], sums_ref[...], 8, 0),
+        ],
+        axis=1,
+    )
     row = 0
-    for sd, sh, sw in BLOCKS_ONE:
-        base = vol[192:] if sd else vol
+    for sd, sh, sw in SHIFTS:
+        base = vol[192:] if sw else vol
         shift = 64 * sd + 8 * sh + sw
         if shift:
             base = pltpu.roll(base, shift, 1)
@@ -89,9 +121,9 @@
         if sw:
             base = jnp.where(q_all[: base.shape[0]] == 0, 0.0, base)
         base = base.astype(jnp.bfloat16)
-        if sh:
-            for md in range(base.shape[0] // 64):
-                x_ref[row : row + 16] = base[md * 64 + 48 : md * 64 + 64]
+        if sd:
+            for mw in range(base.shape[0] // 64):
+                x_ref[row : row + 16] = base[mw * 64 + 48 : mw * 64 + 64]
                 row += 16
         else:
             x_ref[row : row + base.shape[0]] = base
@@ -115,7 +147,7 @@
 
     cot = c_ref[...].astype(jnp.float32)
     moved = {}
-    for sd, sh, sw in BLOCKS_ONE:
+    for sd, sh, sw in SHIFTS:
         shift = 64 * sd + 8 * sh + sw
         part = pltpu.roll(cot, 256 - shift, 1) if shift else cot
         part = part[:, :CELLS]
@@ -239,9 +271,9 @@
         return dot(system["high"][...], high) + (
             dot(system["high"][...], low) + dot(system["low"][...], high)
         )
-    return dot(high, system["high"][...]) + (
-        dot(low, system["high"][...]) + dot(high, system["low"][...])
-    )
+    rows = high.shape[0]
+    both = dot(jnp.concatenate([high, low], axis=0), system["high"][...])
+    return both[:rows] + (both[rows:] + dot(high, system["low"][...]))
 
 
 def conjugate_gradients(systems):
@@ -390,24 +422,20 @@
     return jax.ShapeDtypeStruct(shape, jnp.bfloat16)
 
 
-def to_phases(volume):
-    parts = volume.reshape(4, volume.shape[1] // 4, 4, 8, 4, 8, 4)
-    return parts.transpose(2, 4, 6, 0, 1, 3, 5).reshape(256, -1)
-
-
 def on_device(volume, cotangent, conv_one, conv_two):
     local = volume[0]
     cot = cotangent[0]
-    phases = to_phases(local)
-    halo = passed_along(phases[:, PLANE:], "space", 1)
+    halo = passed_along(local[:, 4:], "space", 1).reshape(-1, 32)
     cot_halo = passed_along(cot[:, :PLANE], "space", -1)
-    vol = jnp.concatenate([jnp.zeros((256, PLANE), jnp.bfloat16), halo, phases], axis=1)
     cot_ext = jnp.concatenate([cot, cot_halo, jnp.zeros((64, PLANE), jnp.bfloat16)], axis=1)
     w1 = jnp.pad(conv_one.reshape(32, 108), ((0, 0), (0, 20)))
     taps_two = conv_two.reshape(64, 32, 27)
     w2 = taps_two.transpose(0, 2, 1).reshape(64, 864)
     w2t = taps_two.transpose(2, 1, 0).reshape(864, 64)
     sel = jnp.asarray(selection(), jnp.bfloat16)
+    spread = jnp.asarray(column_spread(), jnp.bfloat16)
+    row_sums_own = jnp.asarray(row_sums(8), jnp.bfloat16)
+    row_sums_halo = jnp.asarray(row_sums(4), jnp.bfloat16)
     out_two, e1, block_a, block_b, small = pl.pallas_call(
         local_kernel,
         out_shape=(bf16(64, CELLS), bf16(256, CELLS), bf16(HALF, CELLS), bf16(320 - HALF, CELLS), f32(SUMS, 128)),
@@ -416,7 +444,7 @@
             pltpu.VMEM((1024, 256), jnp.bfloat16),
             pltpu.VMEM((864, CELLS), jnp.bfloat16),
         ],
-    )(vol, cot_ext, sel, w1, w2, w2t)
+    )(local.reshape(-1, 32), halo, spread, row_sums_own, row_sums_halo, cot_ext, sel, w1, w2, w2t)
     grad_pre = e1.reshape(2, 2, 2, 32, 2, 8, 8).transpose(3, 4, 0, 5, 1, 6, 2).reshape(32, 1024)
 
     counts = (lax.axis_size("dp"), lax.axis_size("space"))

time: 131 us -> 112 us (0.85); the launches traced: 132 us -> 112 us
  Pallas kernels: 106 us -> 93.9 us
  local copies, waits for them, and re-layouts: 18.5 us -> 11.9 us
  waiting for transfers between devices: 2.07 us -> 0.01 us
    pallas_call x1, Pallas kernels: 65.4 us -> 51.6 us  [on_device(): pl.pallas_call(lambda *refs: solve_kernel(plan, counts, *refs), out_shape...]
    transpose x1 -> x0, local copies, waits for them, and re-layouts: 7.65 us -> none  [to_phases(): return parts.transpose(2, 4, 6, 0, 1, 3, 5).reshape(256, -1)]
    another operation x1 -> x0, local copies, waits for them, and re-layouts: 2.56 us -> none  [to_phases(): parts = volume.reshape(4, volume.shape[1] // 4, 4, 8, 4, 8, 4)]
    ppermute x2, waiting for transfers between devices: 2.07 us -> 0.01 us  [passed_along(): lax.ppermute(value, axis, [(source, source + steps) for source in range(l...]
    unnamed x12 -> x4, local copies, waits for them, and re-layouts: 0.79 us -> 2.17 us
  transfers between devices with their start and end apart: 2 -> 2, of which waited for: 1 -> 0; matrix products, arithmetic and copies ran while one was open for 2% -> 5% of each run, Pallas kernels for 0% -> 0%
where the time goes in v3:
time: 112 us
  Pallas kernels  93.9 us (84%)
  local copies, waits for them, and re-layouts  11.9 us (11%)
  starting transfers between devices  4.33 us (4%)
  other arithmetic  1.34 us (1%)
    pallas_call x1, Pallas kernels, on_device(): pl.pallas_call(lambda *refs: solve_kernel(plan, counts, *refs), out_shape...  51.6 us
    pallas_call x1, Pallas kernels, on_device(): pl.pallas_call(lambda *refs: exchange_kernel(plan, *refs), out_shape=(bf1...  36.4 us
    pallas_call x1, Pallas kernels, on_device(): pl.pallas_call(local_kernel, out_shape=(bf16(64, CELLS), bf16(256, CELLS)...  5.82 us
    ppermute x2, starting transfers between devices, passed_along(): lax.ppermute(value, axis, [(source, source + steps) for source in range(l...  4.33 us
  transfers between devices with their start and end apart: 2, of which 0 were waited for; matrix products, arithmetic and copies ran while one was open for 5% of the time, Pallas kernels for 0%

profile of v3, /device:TPU:0, one launch (start us, length us, event | category | flops | bytes accessed | tf_op | source)
XLA Modules:
  0.0 112.1 jit_solution(11472372159032213436)
XLA Ops:
  0.6 1.3 %collective-permute-start.1 = (bf16[64,64]{1,0:T(8,128)(2,1)}, bf16[64,64]{1,0:T(8,128)(2,1)S(1)}, u32[]{:S(2)}, u32[]{:S(2)}) collective-permute-start(bf16[64,64]{1,0:T(8,128)(2,1)} %bitcast.34), channel_id=1, source_target_pairs={{1,0},{2,1},{3,2},{5,4},{6,5},{7,6},{9,8},{10,9},{11,10},{13,12},{... | collective-permute-start | bytes 24584 | tf_op jit(solution)/shard_map/ppermute | solution.py:414
  1.9 0.9 slice.12
  2.9 3.0 %collective-permute-start = (bf16[4,4,32,32]{3,2,1,0:T(8,128)(2,1)S(1)}, bf16[4,4,32,32]{3,2,1,0:T(8,128)(2,1)S(1)}, u32[]{:S(2)}, u32[]{:S(2)}) collective-permute-start(bf16[4,4,32,32]{3,2,1,0:T(8,128)(2,1)S(1)} %slice.12), channel_id=1, source_target_pairs={{0,1},{1,2},{2,3},{4,5},{5,6},{6,7},{8,9},{9,10},{10,11},{12,13},{... | collective-permute-start | bytes 98312 | tf_op jit(solution)/shard_map/ppermute | solution.py:414
  5.9 0.8 copy.15
  6.7 0.1 copy.16
  6.8 1.7 %copy.17.w2_ref = bf16[64,864]{1,0:T(8,128)(2,1)} copy(bf16[64,864]{0,1:T(8,128)(2,1)} %bitcast.28) | data formatting | bytes 221184 | tf_op jit(solution)/shard_map/reshape | solution.py:433
  8.5 0.6 pad.4.w1_ref
  9.1 0.1 pad.7.clone
  9.2 0.0 collective-permute-done.1
  9.2 1.3 %maximum_maximum_fusion.c_ref = bf16[64,256]{1,0:T(8,128)(2,1)} fusion(bf16[64,64]{1,0:T(8,128)(2,1)S(1)} %collective-permute-done.1, bf16[64,128]{1,0:T(8,128)(2,1)} %bitcast.35, bf16[256]{0:T(256)(128)(2,1)S(1)} %pad.7.clone), kind=kLoop, calls=%fused_computation | loop fusion | flops 98304 | bytes 57856 | tf_op jit(solution)/shard_map/concatenate | solution.py:430
  10.5 0.0 collective-permute-done
  10.5 0.0 copy-start
  10.5 0.7 copy-done
  11.2 5.8 %shard_map.111 = (bf16[64,128]{1,0:T(8,128)(2,1)}, bf16[256,128]{1,0:T(8,128)(2,1)}, bf16[160,128]{1,0:T(8,128)(2,1)}, bf16[160,128]{1,0:T(8,128)(2,1)}, f32[192,128]{1,0:T(8,128)}) custom-call(bf16[1024,32]{1,0:T(8,128)(2,1)} %bitcast.31, bf16[512,32]{1,0:T(8,128)(2,1)} %bitcast.32, bf16[32,512]{1,0:T(8,128)(2,1)} %constant.13.clone.spread_ref, ...), custom_call_target="tpu_custom_call" | custom-call | tf_op jit(solution)/shard_map/pallas_call | solution.py:439
  17.0 0.9 copy.18
  17.9 0.2 reshape.40
  18.1 0.2 copy.19
  18.3 0.8 copy.22
  19.1 36.4 %shard_map.112 = (bf16[32,160,128]{2,1,0:T(8,128)(2,1)}, bf16[32,160,128]{2,1,0:T(8,128)(2,1)}, f32[192,128]{1,0:T(8,128)}) custom-call(bf16[160,128]{1,0:T(8,128)(2,1)} %get-tuple-element.16.refs_0_, bf16[160,128]{1,0:T(8,128)(2,1)} %get-tuple-element.17.refs_1_, f32[192,128]{1,0:T(8,128)} %get-tuple-element.18.refs_2_), custom_call_target="tpu_custom_call" | custom-call | tf_op jit(solution)/shard_map/pallas_call | solution.py:454
  55.5 51.6 %shard_map.113 = (f32[32,128]{1,0:T(8,128)}, f32[64,864]{1,0:T(8,128)}) custom-call(bf16[32,160,128]{2,1,0:T(8,128)(2,1)} %get-tuple-element.19.refs_0_, bf16[32,160,128]{2,1,0:T(8,128)(2,1)} %get-tuple-element.20.refs_1_, f32[192,128]{1,0:T(8,128)} %get-tuple-element.21.refs_2_), custom_call_target="tpu_custom_call" | custom-call | tf_op jit(solution)/shard_map/pallas_call | solution.py:468
  107.1 1.4 %reshape.41 = f32[3456]{0:T(1024)} reshape(f32[32,108]{1,0:T(8,128)} %bitcast.33) | data formatting | bytes 27648 | tf_op jit(solution)/shard_map/reshape | solution.py:482
  108.5 1.1 %copy.20 = f32[64,864]{0,1:T(8,128)S(1)} copy(f32[64,864]{1,0:T(8,128)} %get-tuple-element.23) | data formatting | bytes 442368 | tf_op jit(solution)/shard_map/pallas_call | solution.py:468
  109.7 1.0 copy.21
  110.7 1.5 %reshape.43 = f32[55296]{0:T(1024)} reshape(f32[64,32,27]{2,1,0:T(8,128)S(1)} %copy.21) | data formatting | bytes 442368 | tf_op jit(solution)/shard_map/reshape | solution.py:483
  (2 shorter events, 0.0 us)
Async XLA Ops:
  0.6 8.6 %collective-permute-start.1 = (bf16[64,64]{1,0:T(8,128)(2,1)}, bf16[64,64]{1,0:T(8,128)(2,1)S(1)}, u32[]{:S(2)}, u32[]{:S(2)}) collective-permute-start(bf16[64,64]{1,0:T(8,128)(2,1)} %bitcast.34), channel_id=1, source_target_pairs={{1,0},{2,1},{3,2},{5,4},{6,5},{7,6},{9,8},{10,9},{11,10},{13,12},{... | collective-permute-start | bytes 24584 | tf_op jit(solution)/shard_map/ppermute | solution.py:414
  2.9 7.7 %collective-permute-start = (bf16[4,4,32,32]{3,2,1,0:T(8,128)(2,1)S(1)}, bf16[4,4,32,32]{3,2,1,0:T(8,128)(2,1)S(1)}, u32[]{:S(2)}, u32[]{:S(2)}) collective-permute-start(bf16[4,4,32,32]{3,2,1,0:T(8,128)(2,1)S(1)} %slice.12), channel_id=1, source_target_pairs={{0,1},{1,2},{2,3},{4,5},{5,6},{6,7},{8,9},{9,10},{10,11},{12,13},{... | collective-permute-start | bytes 98312 | tf_op jit(solution)/shard_map/ppermute | solution.py:414
  10.5 0.7 copy-start
